TPU v7x, 32 devices: a whole 2x2x4 slice. The times are simulated.
32 devices in a mesh: section: 2 (over x), wrow: 4 (over y, core), wcol: 4 (over z).
Axes of the slice: x: 2, y: 2, z: 4, core: 2. Of those that a mesh axis runs over, the one named last changes fastest.
Arguments:
- states: bfloat16 [2, 64, 64, 1536], P(None, 'wrow', 'wcol'), may hold values from -6 to 6
- timesteps: int32 [2], replicated, may hold values from 0 to 999, as said below
- shifts: int32 [2, 2], P('section'), may hold values from 1 to 4
- qkv_weight: bfloat16 [2, 1536, 2304], P('section', None, 'wcol'), may hold values from -0.15625 to 0.15625
- out_weight: bfloat16 [2, 768, 1536], P('section', None, 'wcol'), may hold values from -0.21875 to 0.21875
- mod_weight: bfloat16 [2, 256, 4608], P('section', None, 'wcol'), may hold values from -0.375 to 0.375
Outputs:
- layer_states: bfloat16 [2, 2, 64, 64, 1536], P('section', None, 'wrow', 'wcol')
Inputs may be any that keep to these rules, and one draw needn't show every extreme that they name: The 2 timesteps are distinct.
All inputs are finite; a program needn't handle non-finite values.
Results may differ from a plain program's by a relative error of at most 0.0053.
Values may be sent and summed in bfloat16 or wider, within the bound.
No kernel may reach another device: no remote copies, remote signals or barrier semaphores. Data moves between devices by JAX's collectives and lax.ppermute only.
A program may use at most 128 MiB of HBM per device.

v0:
```python
import math
import jax
import jax.numpy as jnp
from jax import lax
from jax.sharding import PartitionSpec as P

HEADS = 6
HD = 128
TEMB = 256
WIN = 8
MB = 2
epsilon = 1e-06


def passed_along(shard, axis, by):
    devices = lax.axis_size(axis)
    return lax.ppermute(shard, axis, [(i, (i + by) % devices) for i in range(devices)])


def from_behind(shard, axis, by):
    devices = lax.axis_size(axis)
    pairs = [(i, i + by) for i in range(devices) if 0 <= i + by < devices]
    return lax.ppermute(shard, axis, pairs)


def sinusoid(moments, entries):
    half_count = entries // 2
    frequency = jnp.exp(-math.log(10000.0) * jnp.arange(half_count, dtype=jnp.float32) / half_count)
    angles = moments.astype(jnp.float32)[:, None] * frequency[None, :]
    return jnp.concatenate([jnp.cos(angles), jnp.sin(angles)], axis=1)


def layer_norm(region):
    values = region.astype(jnp.float32)
    center = values - jnp.mean(values, axis=-1, keepdims=True)
    spread = jnp.mean(center * center, axis=-1, keepdims=True)
    return center * lax.rsqrt(spread + epsilon)


def window_attention(triples):
    tile_rows, tile_cols, feature_width = triples.shape
    windowed = triples.reshape(tile_rows // WIN, WIN, tile_cols // WIN, WIN, 3, HEADS, HD)
    windowed = windowed.transpose(4, 0, 2, 5, 1, 3, 6).reshape(
        3, tile_rows // WIN * (tile_cols // WIN), HEADS, WIN * WIN, HD
    )
    scores = jnp.einsum(
        "nhqd,nhkd->nhqk", windowed[0], windowed[1], preferred_element_type=jnp.float32
    ) * HD ** (-0.5)
    weights = jnp.exp(scores)
    probabilities = (weights / jnp.sum(weights, axis=-1, keepdims=True)).astype(jnp.bfloat16)
    attended = jnp.einsum(
        "nhqk,nhkd->nhqd", probabilities, windowed[2], preferred_element_type=jnp.float32
    ).astype(jnp.bfloat16)
    attended = attended.reshape(tile_rows // WIN, tile_cols // WIN, HEADS, WIN, WIN, HD).transpose(
        0, 3, 1, 4, 2, 5
    )
    return attended.reshape(tile_rows, tile_cols, HEADS * HD)


def project(region, matrix):
    tile_rows, tile_cols, feature_width = region.shape
    product = jnp.dot(
        region.reshape(tile_rows * tile_cols, feature_width),
        matrix,
        preferred_element_type=jnp.float32,
    )
    return product.reshape(tile_rows, tile_cols, -1)


def splice(region, border, amount, direction, margin, axis_index):
    if direction > 0:
        longer = jnp.concatenate([region, border], axis=axis_index)
        offset = amount
    else:
        longer = jnp.concatenate([border, region], axis=axis_index)
        offset = margin - amount
    return lax.dynamic_slice_in_dim(longer, offset, region.shape[axis_index], axis_index)


def wrap_rim(region, row_shift, col_shift, direction):
    margin = WIN // 2
    if direction > 0:
        border = region[:margin]
    else:
        border = region[region.shape[0] - margin :]
    border = passed_along(border, "wrow", -direction)
    region = splice(region, border, row_shift, direction, margin, 0)
    if direction > 0:
        border = region[:, :margin]
    else:
        border = region[:, region.shape[1] - margin :]
    border = passed_along(border, "wcol", -direction)
    return splice(region, border, col_shift, direction, margin, 1)


def shifted_layer(inputs, modulation, row_shift, col_shift, qkv_matrix, out_matrix):
    feature_width = inputs.shape[-1]
    mod_shift = modulation[:feature_width]
    mod_scale = modulation[feature_width : 2 * feature_width]
    mod_gate = modulation[2 * feature_width :]
    normed = (layer_norm(inputs) * (1.0 + mod_scale) + mod_shift).astype(jnp.bfloat16)
    rolled = wrap_rim(normed, row_shift, col_shift, 1)
    triples = project(rolled, qkv_matrix).astype(jnp.bfloat16)
    attended = window_attention(triples)
    projection = project(attended, out_matrix).astype(jnp.bfloat16)
    projection = wrap_rim(projection, row_shift, col_shift, -1).astype(jnp.float32)
    return (inputs.astype(jnp.float32) + mod_gate * projection).astype(jnp.bfloat16)


def slice_part(matrix, position, across):
    piece_width = matrix.shape[1] // across
    return lax.dynamic_slice_in_dim(matrix, position * piece_width, piece_width, 1)


def regroup(matrix, across, along):
    leading = matrix.shape[0]
    piece_width = matrix.shape[1] // (across * along)
    return (
        matrix.reshape(leading, across, along, piece_width)
        .transpose(0, 2, 1, 3)
        .reshape(leading, -1)
    )


def per_device(states, timesteps, shifts, qkv_weight, out_weight, mod_weight):
    embedding = jax.nn.silu(sinusoid(timesteps, TEMB)).astype(jnp.bfloat16)
    mod_part = jnp.dot(embedding, mod_weight[0], preferred_element_type=jnp.float32).astype(
        jnp.bfloat16
    )
    across = lax.axis_size("wrow")
    along = lax.axis_size("wcol")
    position = lax.axis_index("wrow")
    gathered = (
        lax.all_gather(
            slice_part(qkv_weight[0], position, across), ("wrow", "wcol"), axis=1, tiled=True
        ),
        lax.all_gather(
            slice_part(out_weight[0], position, across), ("wrow", "wcol"), axis=1, tiled=True
        ),
        lax.all_gather(
            slice_part(mod_part, position, across), ("wrow", "wcol"), axis=1, tiled=True
        ),
    )
    qkv_full = regroup(gathered[0], across, along)
    out_full = regroup(gathered[1], across, along)
    modulations = regroup(gathered[2], across, along)
    section_index = lax.axis_index("section")
    moments = MB + lax.axis_size("section") - 1
    row_shift = shifts[0, 0]
    col_shift = shifts[0, 1]
    incoming = jnp.zeros_like(states[0])
    results = jnp.zeros_like(states)
    for moment in range(moments):
        member = moment - section_index
        batch_slot = jnp.clip(member, 0, MB - 1)
        block_input = jnp.where(section_index == 0, states[min(moment, MB - 1)], incoming)
        modulation = lax.dynamic_index_in_dim(modulations, batch_slot, 0, keepdims=False).astype(
            jnp.float32
        )
        outgoing = shifted_layer(block_input, modulation, row_shift, col_shift, qkv_full, out_full)
        active = (member >= 0) & (member < MB)
        updated = lax.dynamic_update_index_in_dim(results, outgoing, batch_slot, 0)
        results = jnp.where(active, updated, results)
        if moment + 1 < moments:
            incoming = from_behind(outgoing, "section", 1)
    return results[None]


def solution(mesh):
    in_specs = (
        P(None, "wrow", "wcol", None),
        P(),
        P("section", None),
        P("section", None, "wcol"),
        P("section", None, "wcol"),
        P("section", None, "wcol"),
    )
    out_specs = P("section", None, "wrow", "wcol", None)
    return jax.shard_map(
        per_device, mesh=mesh, in_specs=in_specs, out_specs=out_specs, check_vma=False
    )
```

profile of v0, /device:TPU:0, one launch (start us, length us, event | category | flops | bytes accessed | tf_op | source)
XLA Modules:
  0.0 278.9 jit_solution(11938716838353509522)
XLA Ops:
  6.5 1.3 constant_dynamic-slice_fusion
  11.0 34.5 %all-gather.2 = bf16[16,288,2]{1,2,0:T(2,128)(2,1)S(1)} all-gather(bf16[1,288,2]{1,2,0:T(2,128)(2,1)S(1)} %fusion.62), channel_id=1, replica_groups=mesh['section'=2,'wrow'=4,'wcol'=4] {'wrow','wcol'}, dimensions={0}, use_global_device_ids=true | all-gather | bytes 19584 | tf_op jit(solution)/shard_map/all_gather | solution.py:140
  51.7 1.3 fusion.31
  55.1 3.3 %copy.85 = bf16[768,4,4,96]{0,3,2,1:T(8,128)(2,1)} copy(bf16[768,4,4,96]{0,3,1,2:T(8,128)(2,1)} %bitcast.135) | data formatting | bytes 4718592 | tf_op jit(solution)/shard_map/transpose | solution.py:120
  58.3 63.5 %all-gather.6.cloned.1.call-done = bf16[1,1536,2304]{1,2,0:T(8,128)(2,1)} async-done(((bf16[1,1536,144]{1,2,0:T(8,128)(2,1)}), bf16[1,1536,2304]{1,2,0:T(8,128)(2,1)}) %all-gather.6.cloned.1.call-update) | async-done | bytes 7077904 | tf_op jit(solution)/shard_map/all_gather | solution.py:134
  121.8 3.6 %copy.77 = bf16[1536,4,4,144]{0,3,2,1:T(8,128)(2,1)S(1)} copy(bf16[1536,4,4,144]{0,3,1,2:T(8,128)(2,1)} %bitcast.131) | data formatting | bytes 14155776 | tf_op jit(solution)/shard_map/transpose | solution.py:120
  125.4 2.4 convolution_convert_fusion.2
  129.5 2.5 convolution_convert_fusion.5
  133.6 3.6 %collective-permute-done.2 = bf16[4,16,1536]{2,1,0:T(8,128)(2,1)S(1)} collective-permute-done((bf16[4,16,1536]{2,1,0:T(8,128)(2,1)S(1)}, bf16[4,16,1536]{2,1,0:T(8,128)(2,1)S(1)}, u32[]{:S(2)}, u32[]{:S(2)}) %collective-permute-start.2) | collective-permute-done | bytes 196640 | tf_op jit(solution)/shard_map/ppermute | solution.py:17
  138.3 1.6 collective-permute-start.3
  141.2 4.6 %collective-permute-done.3 = bf16[16,4,1536]{2,1,0:T(4,128)(2,1)S(1)} collective-permute-done((bf16[16,4,1536]{2,1,0:T(4,128)(2,1)S(1)}, bf16[16,4,1536]{2,1,0:T(4,128)(2,1)S(1)}, u32[]{:S(2)}, u32[]{:S(2)}) %collective-permute-start.3) | collective-permute-done | bytes 196640 | tf_op jit(solution)/shard_map/ppermute | solution.py:17
  146.0 2.0 bitcast_dynamic-update-slice_fusion
  148.1 3.4 %collective-permute-start.4 = (bf16[16,16,1536]{2,1,0:T(8,128)(2,1)S(1)}, bf16[16,16,1536]{2,1,0:T(8,128)(2,1)S(1)}, u32[]{:S(2)}, u32[]{:S(2)}) collective-permute-start(bf16[16,16,1536]{2,1,0:T(8,128)(2,1)S(1)} %get-tuple-element.21), channel_id=1, source_target_pairs={{0,16},{1,17},{2,18},{3,19},{4,20},{5,21},{6,22},{7,23},{8,24},{9,... | collective-permute-start | bytes 2359304 | tf_op jit(solution)/shard_map/ppermute | solution.py:23
  151.5 13.9 %collective-permute-done.4 = bf16[16,16,1536]{2,1,0:T(8,128)(2,1)S(1)} collective-permute-done((bf16[16,16,1536]{2,1,0:T(8,128)(2,1)S(1)}, bf16[16,16,1536]{2,1,0:T(8,128)(2,1)S(1)}, u32[]{:S(2)}, u32[]{:S(2)}) %collective-permute-start.4) | collective-permute-done | bytes 786464 | tf_op jit(solution)/shard_map/ppermute | solution.py:23
  166.6 3.2 %collective-permute-done.5 = bf16[4,16,1536]{2,1,0:T(8,128)(2,1)S(1)} collective-permute-done((bf16[4,16,1536]{2,1,0:T(8,128)(2,1)S(1)}, bf16[4,16,1536]{2,1,0:T(8,128)(2,1)S(1)}, u32[]{:S(2)}, u32[]{:S(2)}) %collective-permute-start.5) | collective-permute-done | bytes 196640 | tf_op jit(solution)/shard_map/ppermute | solution.py:17
  170.6 6.1 %collective-permute-done.6 = bf16[16,4,1536]{2,1,0:T(4,128)(2,1)S(1)} collective-permute-done((bf16[16,4,1536]{2,1,0:T(4,128)(2,1)S(1)}, bf16[16,4,1536]{2,1,0:T(4,128)(2,1)S(1)}, u32[]{:S(2)}, u32[]{:S(2)}) %collective-permute-start.6) | collective-permute-done | bytes 196640 | tf_op jit(solution)/shard_map/ppermute | solution.py:17
  176.7 5.4 %convolution_convert_fusion.1 = bf16[16,16,2304]{2,1,0:T(8,128)(2,1)S(1)} fusion(bf16[1536,2304,1]{0,1,2:T(8,128)(2,1)} %bitcast.129, s32[]{:T(128)S(6)} %select_n.93, bf16[16,16,1536]{2,1,0:T(8,128)(2,1)S(1)} %fusion.29, bf16[16,4,1536]{2,1,0:T(4,128)(2,1)S(1)} %collective-permute-done.6), kind=kOutput, calls=%fused_computation.1 | convolution fusion | flops 1814102016 | bytes 9240580 | tf_op jit(solution)/shard_map/dot_general | solution.py:62
  184.5 2.6 convolution_convert_fusion.7
  188.1 2.5 convolution_convert_fusion.4
  191.8 3.9 %collective-permute-done.7 = bf16[4,16,1536]{2,1,0:T(8,128)(2,1)S(1)} collective-permute-done((bf16[4,16,1536]{2,1,0:T(8,128)(2,1)S(1)}, bf16[4,16,1536]{2,1,0:T(8,128)(2,1)S(1)}, u32[]{:S(2)}, u32[]{:S(2)}) %collective-permute-start.7) | collective-permute-done | bytes 196640 | tf_op jit(solution)/shard_map/ppermute | solution.py:17
  197.6 9.1 %collective-permute-done.8 = bf16[16,4,1536]{2,1,0:T(4,128)(2,1)S(1)} collective-permute-done((bf16[16,4,1536]{2,1,0:T(4,128)(2,1)}, bf16[16,4,1536]{2,1,0:T(4,128)(2,1)S(1)}, u32[]{:S(2)}, u32[]{:S(2)}) %collective-permute-start.8) | collective-permute-done | bytes 196640 | tf_op jit(solution)/shard_map/ppermute | solution.py:17
  206.7 2.3 fusion.45
  209.0 4.4 %collective-permute-start.9 = (bf16[16,16,1536]{2,1,0:T(8,128)(2,1)S(1)}, bf16[16,16,1536]{2,1,0:T(8,128)(2,1)S(1)}, u32[]{:S(2)}, u32[]{:S(2)}) collective-permute-start(bf16[16,16,1536]{2,1,0:T(8,128)(2,1)S(1)} %get-tuple-element.17), channel_id=1, source_target_pairs={{0,16},{1,17},{2,18},{3,19},{4,20},{5,21},{6,22},{7,23},{8,24},{9,... | collective-permute-start | bytes 2359304 | tf_op jit(solution)/shard_map/ppermute | solution.py:23
  213.5 16.3 %collective-permute-done.9 = bf16[16,16,1536]{2,1,0:T(8,128)(2,1)S(1)} collective-permute-done((bf16[16,16,1536]{2,1,0:T(8,128)(2,1)S(1)}, bf16[16,16,1536]{2,1,0:T(8,128)(2,1)S(1)}, u32[]{:S(2)}, u32[]{:S(2)}) %collective-permute-start.9) | collective-permute-done | bytes 786464 | tf_op jit(solution)/shard_map/ppermute | solution.py:23
  231.0 3.2 %collective-permute-done.10 = bf16[4,16,1536]{2,1,0:T(8,128)(2,1)S(1)} collective-permute-done((bf16[4,16,1536]{2,1,0:T(8,128)(2,1)S(1)}, bf16[4,16,1536]{2,1,0:T(8,128)(2,1)S(1)}, u32[]{:S(2)}, u32[]{:S(2)}) %collective-permute-start.10) | collective-permute-done | bytes 196640 | tf_op jit(solution)/shard_map/ppermute | solution.py:17
  234.8 7.0 %collective-permute-done.11 = bf16[16,4,1536]{2,1,0:T(4,128)(2,1)S(1)} collective-permute-done((bf16[16,4,1536]{2,1,0:T(4,128)(2,1)S(1)}, bf16[16,4,1536]{2,1,0:T(4,128)(2,1)S(1)}, u32[]{:S(2)}, u32[]{:S(2)}) %collective-permute-start.11) | collective-permute-done | bytes 196640 | tf_op jit(solution)/shard_map/ppermute | solution.py:17
  241.8 5.4 %convolution_convert_fusion = bf16[16,16,2304]{2,1,0:T(8,128)(2,1)S(1)} fusion(bf16[1536,2304,1]{0,1,2:T(8,128)(2,1)} %bitcast.130, s32[]{:T(128)S(6)} %select_n.93, bf16[16,16,1536]{2,1,0:T(8,128)(2,1)S(1)} %fusion.27, bf16[16,4,1536]{2,1,0:T(4,128)(2,1)S(1)} %collective-permute-done.11), kind=kOutput, calls=%fused_computation | convolution fusion | flops 1814102016 | bytes 9240580 | tf_op jit(solution)/shard_map/dot_general | solution.py:62
  249.5 2.6 convolution_convert_fusion.6
  253.2 2.5 convolution_convert_fusion.3
  255.8 5.1 %collective-permute-done.12 = bf16[4,16,1536]{2,1,0:T(8,128)(2,1)S(1)} collective-permute-done((bf16[4,16,1536]{2,1,0:T(8,128)(2,1)S(1)}, bf16[4,16,1536]{2,1,0:T(8,128)(2,1)S(1)}, u32[]{:S(2)}, u32[]{:S(2)}) %collective-permute-start.12) | collective-permute-done | bytes 196640 | tf_op jit(solution)/shard_map/ppermute | solution.py:17
  263.2 6.4 %collective-permute-done.13 = bf16[16,4,1536]{2,1,0:T(4,128)(2,1)} collective-permute-done((bf16[16,4,1536]{2,1,0:T(4,128)(2,1)S(1)}, bf16[16,4,1536]{2,1,0:T(4,128)(2,1)}, u32[]{:S(2)}, u32[]{:S(2)}) %collective-permute-start.13) | collective-permute-done | bytes 196640 | tf_op jit(solution)/shard_map/ppermute | solution.py:17
  269.6 2.5 fusion.44
  (124 shorter events, 26.8 us)
Async XLA Ops:
  6.5 2.2 copy-start
  6.5 3.0 %copy-start.17 = (s32[2]{0:T(128)S(1)}, s32[2]{0:T(128)}, u32[]{:S(2)}) copy-start(s32[2]{0:T(128)} %param.7) | copy-start | bytes 28
  6.5 48.5 %all-gather.8.cloned.1.call-start = ((), (), s32[]{:S(2)}) async-start(), calls=%async_computation.1 | async-start | bytes 2506752 | tf_op jit(solution)/shard_map/all_gather | solution.py:137
  6.5 40.0 %copy-start.1 = (bf16[2,16,16,1536]{3,2,1,0:T(8,128)(2,1)S(1)}, bf16[2,16,16,1536]{3,2,1,0:T(8,128)(2,1)}, u32[]{:S(2)}) copy-start(bf16[2,16,16,1536]{3,2,1,0:T(8,128)(2,1)} %param.6) | copy-start | bytes 4718596
  8.7 113.2 %all-gather.6.cloned.1.call-start = ((), (), s32[]{:S(2)}) async-start(), calls=%async_computation | async-start | bytes 7520256 | tf_op jit(solution)/shard_map/all_gather | solution.py:134
  46.8 1.7 copy-start.16
  47.6 0.9 copy-start.9
  48.5 3.2 %collective-permute-start = (bf16[4,16,1536]{2,1,0:T(8,128)(2,1)S(1)}, bf16[4,16,1536]{2,1,0:T(8,128)(2,1)S(1)}, u32[]{:S(2)}, u32[]{:S(2)}) collective-permute-start(bf16[4,16,1536]{2,1,0:T(8,128)(2,1)S(1)} %slice.176), channel_id=1, source_target_pairs={{0,12},{4,0},{8,4},{12,8},{1,13},{5,1},{9,5},{13,9},{2,14},{6,2},{... | collective-permute-start | bytes 589832 | tf_op jit(solution)/shard_map/ppermute | solution.py:17
  53.1 72.4 %collective-permute-start.1 = (bf16[16,4,1536]{2,1,0:T(4,128)(2,1)S(1)}, bf16[16,4,1536]{2,1,0:T(4,128)(2,1)S(1)}, u32[]{:S(2)}, u32[]{:S(2)}) collective-permute-start(bf16[16,4,1536]{2,1,0:T(4,128)(2,1)S(1)} %slice.177), channel_id=1, source_target_pairs={{0,3},{1,0},{2,1},{3,2},{4,7},{5,4},{6,5},{7,6},{8,11},{9,8},{10,9... | collective-permute-start | bytes 589832 | tf_op jit(solution)/shard_map/ppermute | solution.py:17
  125.4 2.9 %copy-start.7 = (bf16[1536,4,4,144]{0,3,2,1:T(8,128)(2,1)}, bf16[1536,4,4,144]{0,3,2,1:T(8,128)(2,1)S(1)}, u32[]{:S(2)}) copy-start(bf16[1536,4,4,144]{0,3,2,1:T(8,128)(2,1)S(1)} %copy.77) | copy-start | bytes 21233668
  132.0 5.1 %collective-permute-start.2 = (bf16[4,16,1536]{2,1,0:T(8,128)(2,1)S(1)}, bf16[4,16,1536]{2,1,0:T(8,128)(2,1)S(1)}, u32[]{:S(2)}, u32[]{:S(2)}) collective-permute-start(bf16[4,16,1536]{2,1,0:T(8,128)(2,1)S(1)} %slice.181), channel_id=1, source_target_pairs={{0,4},{4,8},{8,12},{12,0},{1,5},{5,9},{9,13},{13,1},{2,6},{6,10},{... | collective-permute-start | bytes 589832 | tf_op jit(solution)/shard_map/ppermute | solution.py:17
  137.3 0.9 copy-start.10
  138.3 7.5 %collective-permute-start.3 = (bf16[16,4,1536]{2,1,0:T(4,128)(2,1)S(1)}, bf16[16,4,1536]{2,1,0:T(4,128)(2,1)S(1)}, u32[]{:S(2)}, u32[]{:S(2)}) collective-permute-start(bf16[16,4,1536]{2,1,0:T(4,128)(2,1)S(1)} %slice.182), channel_id=1, source_target_pairs={{0,1},{1,2},{2,3},{3,0},{4,5},{5,6},{6,7},{7,4},{8,9},{9,10},{10,1... | collective-permute-start | bytes 589832 | tf_op jit(solution)/shard_map/ppermute | solution.py:17
  141.2 4.8 %copy-start.11 = (bf16[16,16,1536]{2,1,0:T(8,128)(2,1)S(1)}, bf16[16,16,1536]{2,1,0:T(8,128)(2,1)}, u32[]{:S(2)}) copy-start(bf16[16,16,1536]{2,1,0:T(8,128)(2,1)} %copy-done.10) | copy-start | bytes 2359300
  146.0 5.5 %copy-start.15 = (f32[1,4608]{1,0:T(1,128)S(1)}, f32[1,4608]{1,0:T(1,128)}, u32[]{:S(2)}) copy-start(f32[1,4608]{1,0:T(1,128)} %get-tuple-element.32) | copy-start | bytes 55300
  146.0 19.4 %copy-start.2 = (bf16[2,16,16,1536]{3,2,1,0:T(8,128)(2,1)S(1)}, bf16[2,16,16,1536]{3,2,1,0:T(8,128)(2,1)}, u32[]{:S(2)}) copy-start(bf16[2,16,16,1536]{3,2,1,0:T(8,128)(2,1)} %param.6) | copy-start | bytes 4718596
  148.1 17.4 %collective-permute-start.4 = (bf16[16,16,1536]{2,1,0:T(8,128)(2,1)S(1)}, bf16[16,16,1536]{2,1,0:T(8,128)(2,1)S(1)}, u32[]{:S(2)}, u32[]{:S(2)}) collective-permute-start(bf16[16,16,1536]{2,1,0:T(8,128)(2,1)S(1)} %get-tuple-element.21), channel_id=1, source_target_pairs={{0,16},{1,17},{2,18},{3,19},{4,20},{5,21},{6,22},{7,23},{8,24},{9,... | collective-permute-start | bytes 2359304 | tf_op jit(solution)/shard_map/ppermute | solution.py:23
  165.7 4.2 %copy-start.4 = (bf16[16,16,1536]{2,1,0:T(8,128)(2,1)}, bf16[16,16,1536]{2,1,0:T(8,128)(2,1)S(1)}, u32[]{:S(2)}) copy-start(bf16[16,16,1536]{2,1,0:T(8,128)(2,1)S(1)} %get-tuple-element.19) | copy-start | bytes 2359300
  166.5 3.2 %collective-permute-start.5 = (bf16[4,16,1536]{2,1,0:T(8,128)(2,1)S(1)}, bf16[4,16,1536]{2,1,0:T(8,128)(2,1)S(1)}, u32[]{:S(2)}, u32[]{:S(2)}) collective-permute-start(bf16[4,16,1536]{2,1,0:T(8,128)(2,1)S(1)} %slice.186), channel_id=1, source_target_pairs={{0,12},{4,0},{8,4},{12,8},{1,13},{5,1},{9,5},{13,9},{2,14},{6,2},{... | collective-permute-start | bytes 589832 | tf_op jit(solution)/shard_map/ppermute | solution.py:17
  170.0 6.7 %collective-permute-start.6 = (bf16[16,4,1536]{2,1,0:T(4,128)(2,1)S(1)}, bf16[16,4,1536]{2,1,0:T(4,128)(2,1)S(1)}, u32[]{:S(2)}, u32[]{:S(2)}) collective-permute-start(bf16[16,4,1536]{2,1,0:T(4,128)(2,1)S(1)} %slice.187), channel_id=1, source_target_pairs={{0,3},{1,0},{2,1},{3,2},{4,7},{5,4},{6,5},{7,6},{8,11},{9,8},{10,9... | collective-permute-start | bytes 589832 | tf_op jit(solution)/shard_map/ppermute | solution.py:17
  190.6 5.1 %collective-permute-start.7 = (bf16[4,16,1536]{2,1,0:T(8,128)(2,1)S(1)}, bf16[4,16,1536]{2,1,0:T(8,128)(2,1)S(1)}, u32[]{:S(2)}, u32[]{:S(2)}) collective-permute-start(bf16[4,16,1536]{2,1,0:T(8,128)(2,1)S(1)} %slice.191), channel_id=1, source_target_pairs={{0,4},{4,8},{8,12},{12,0},{1,5},{5,9},{9,13},{13,1},{2,6},{6,10},{... | collective-permute-start | bytes 589832 | tf_op jit(solution)/shard_map/ppermute | solution.py:17
  197.6 9.1 %collective-permute-start.8 = (bf16[16,4,1536]{2,1,0:T(4,128)(2,1)}, bf16[16,4,1536]{2,1,0:T(4,128)(2,1)S(1)}, u32[]{:S(2)}, u32[]{:S(2)}) collective-permute-start(bf16[16,4,1536]{2,1,0:T(4,128)(2,1)} %slice.192), channel_id=1, source_target_pairs={{0,1},{1,2},{2,3},{3,0},{4,5},{5,6},{6,7},{7,4},{8,9},{9,10},{10,1... | collective-permute-start | bytes 589832 | tf_op jit(solution)/shard_map/ppermute | solution.py:17
  206.7 6.8 %copy-start.14 = (f32[1,4608]{1,0:T(1,128)S(1)}, f32[1,4608]{1,0:T(1,128)}, u32[]{:S(2)}) copy-start(f32[1,4608]{1,0:T(1,128)} %get-tuple-element.31) | copy-start | bytes 55300
  206.7 23.1 %copy-start.3 = (bf16[2,16,16,1536]{3,2,1,0:T(8,128)(2,1)S(1)}, bf16[2,16,16,1536]{3,2,1,0:T(8,128)(2,1)}, u32[]{:S(2)}) copy-start(bf16[2,16,16,1536]{3,2,1,0:T(8,128)(2,1)} %param.6) | copy-start | bytes 4718596
  209.0 20.8 %collective-permute-start.9 = (bf16[16,16,1536]{2,1,0:T(8,128)(2,1)S(1)}, bf16[16,16,1536]{2,1,0:T(8,128)(2,1)S(1)}, u32[]{:S(2)}, u32[]{:S(2)}) collective-permute-start(bf16[16,16,1536]{2,1,0:T(8,128)(2,1)S(1)} %get-tuple-element.17), channel_id=1, source_target_pairs={{0,16},{1,17},{2,18},{3,19},{4,20},{5,21},{6,22},{7,23},{8,24},{9,... | collective-permute-start | bytes 2359304 | tf_op jit(solution)/shard_map/ppermute | solution.py:23
  230.1 4.3 %copy-start.5 = (bf16[16,16,1536]{2,1,0:T(8,128)(2,1)}, bf16[16,16,1536]{2,1,0:T(8,128)(2,1)S(1)}, u32[]{:S(2)}) copy-start(bf16[16,16,1536]{2,1,0:T(8,128)(2,1)S(1)} %get-tuple-element.15) | copy-start | bytes 2359300
  230.9 3.2 %collective-permute-start.10 = (bf16[4,16,1536]{2,1,0:T(8,128)(2,1)S(1)}, bf16[4,16,1536]{2,1,0:T(8,128)(2,1)S(1)}, u32[]{:S(2)}, u32[]{:S(2)}) collective-permute-start(bf16[4,16,1536]{2,1,0:T(8,128)(2,1)S(1)} %slice.196), channel_id=1, source_target_pairs={{0,12},{4,0},{8,4},{12,8},{1,13},{5,1},{9,5},{13,9},{2,14},{6,2},{... | collective-permute-start | bytes 589832 | tf_op jit(solution)/shard_map/ppermute | solution.py:17
  234.4 7.3 %collective-permute-start.11 = (bf16[16,4,1536]{2,1,0:T(4,128)(2,1)S(1)}, bf16[16,4,1536]{2,1,0:T(4,128)(2,1)S(1)}, u32[]{:S(2)}, u32[]{:S(2)}) collective-permute-start(bf16[16,4,1536]{2,1,0:T(4,128)(2,1)S(1)} %slice.197), channel_id=1, source_target_pairs={{0,3},{1,0},{2,1},{3,2},{4,7},{5,4},{6,5},{7,6},{8,11},{9,8},{10,9... | collective-permute-start | bytes 589832 | tf_op jit(solution)/shard_map/ppermute | solution.py:17
  255.7 5.1 %collective-permute-start.12 = (bf16[4,16,1536]{2,1,0:T(8,128)(2,1)S(1)}, bf16[4,16,1536]{2,1,0:T(8,128)(2,1)S(1)}, u32[]{:S(2)}, u32[]{:S(2)}) collective-permute-start(bf16[4,16,1536]{2,1,0:T(8,128)(2,1)S(1)} %slice.201), channel_id=1, source_target_pairs={{0,4},{4,8},{8,12},{12,0},{1,5},{5,9},{9,13},{13,1},{2,6},{6,10},{... | collective-permute-start | bytes 589832 | tf_op jit(solution)/shard_map/ppermute | solution.py:17
  262.0 7.6 %collective-permute-start.13 = (bf16[16,4,1536]{2,1,0:T(4,128)(2,1)S(1)}, bf16[16,4,1536]{2,1,0:T(4,128)(2,1)}, u32[]{:S(2)}, u32[]{:S(2)}) collective-permute-start(bf16[16,4,1536]{2,1,0:T(4,128)(2,1)S(1)} %slice.202), channel_id=1, source_target_pairs={{0,1},{1,2},{2,3},{3,0},{4,5},{5,6},{6,7},{7,4},{8,9},{9,10},{10,1... | collective-permute-start | bytes 589832 | tf_op jit(solution)/shard_map/ppermute | solution.py:17
  262.0 7.6 %copy-start.6 = (bf16[16,16,1536]{2,1,0:T(8,128)(2,1)S(1)}, bf16[16,16,1536]{2,1,0:T(8,128)(2,1)}, u32[]{:S(2)}) copy-start(bf16[16,16,1536]{2,1,0:T(8,128)(2,1)} %copy-done.5) | copy-start | bytes 2359300
  262.0 7.5 %copy-start.13 = (bf16[16,16,1536]{2,1,0:T(8,128)(2,1)S(1)}, bf16[16,16,1536]{2,1,0:T(8,128)(2,1)}, u32[]{:S(2)}) copy-start(bf16[16,16,1536]{2,1,0:T(8,128)(2,1)} %copy-done.12) | copy-start | bytes 2359300
  (2 other events, 1.8 us)
Sparse Core Ops, SparseCore 0:
  9.6 45.0 all-gather.7
  57.0 64.7 all-gather.5
where the time goes:
time: 280 us; the launch traced here: 279 us
  waiting for transfers between devices  147 us (52%)
  blocking collectives  34.5 us (12%)
  matrix products  30.1 us (11%)
  local copies, waits for them, and re-layouts  22.3 us (8%)
  between operations  20.4 us (7%)
  other arithmetic  12.9 us (5%)
  starting transfers between devices  12.2 us (4%)
    all_gather x1, waiting for transfers between devices, per_device(): lax.all_gather(slice_part(qkv_weight[0], position, across), ('wrow', 'wco...  63.5 us
    ppermute x12, waiting for transfers between devices, passed_along(): lax.ppermute(shard, axis, [(i, (i + by) % devices) for i in range(devices)])  52.9 us
    all_gather x1, blocking collectives, per_device(): lax.all_gather(slice_part(mod_part, position, across), ('wrow', 'wcol'),...  34.5 us
    ppermute x2, waiting for transfers between devices, from_behind(): return lax.ppermute(shard, axis, pairs)  30.1 us
    dot_general x6, matrix products, project(): jnp.dot(region.reshape(tile_rows * tile_cols, feature_width), matrix, pre...  20.5 us
    ppermute x2, starting transfers between devices, from_behind(): return lax.ppermute(shard, axis, pairs)  7.86 us
    transpose x2, local copies, waits for them, and re-layouts, regroup(): return matrix.reshape(leading, across, along, piece_width).transpose(0, 2...  6.89 us
    select_n x3, other arithmetic, per_device(): results = jnp.where(active, updated, results)  6.86 us
  transfers between devices with their start and end apart: 16, of which 14 were waited for; matrix products, arithmetic and copies ran while one was open for 5% of the time, Pallas kernels for 0%

commit v1 on v0

--- a/solution.py
+++ b/solution.py
@@ -10,6 +10,18 @@
 WIN = 8
 MB = 2
 epsilon = 1e-06
+
+
+def collect(shard, axis, dim):
+    ways, here = (lax.axis_size(axis), lax.axis_index(axis))
+    grown, reach = (shard, 1)
+    while reach < ways:
+        theirs = lax.ppermute(grown, axis, [(d, d ^ reach) for d in range(ways)])
+        mine_first = jnp.concatenate([grown, theirs], axis=dim)
+        theirs_first = jnp.concatenate([theirs, grown], axis=dim)
+        grown = jnp.where(here & reach == 0, mine_first, theirs_first)
+        reach = 2 * reach
+    return grown
 
 
 def passed_along(shard, axis, by):
@@ -131,9 +143,7 @@
     along = lax.axis_size("wcol")
     position = lax.axis_index("wrow")
     gathered = (
-        lax.all_gather(
-            slice_part(qkv_weight[0], position, across), ("wrow", "wcol"), axis=1, tiled=True
-        ),
+        collect(slice_part(qkv_weight[0], position, across), ("wrow", "wcol"), 1),
         lax.all_gather(
             slice_part(out_weight[0], position, across), ("wrow", "wcol"), axis=1, tiled=True
         ),

time: 280 us -> 330 us (1.18)
  waiting for transfers between devices: 147 us -> 179 us
  other arithmetic: 12.9 us -> 24.7 us
  starting transfers between devices: 12.2 us -> 21.5 us
    all_gather x1 -> x0, waiting for transfers between devices: 63.5 us -> none  [per_device(): lax.all_gather(slice_part(qkv_weight[0], position, across), ('wrow', 'wco...]
    ppermute x0 -> x4, waiting for transfers between devices: none -> 49.9 us  [collect(): theirs = lax.ppermute(grown, axis, [(d, d ^ reach) for d in range(ways)])]
    ppermute x12, waiting for transfers between devices: 52.9 us -> 98.7 us  [passed_along(): lax.ppermute(shard, axis, [(i, (i + by) % devices) for i in range(devices)])]
    select_n x0 -> x4, other arithmetic: none -> 8.76 us  [collect(): grown = jnp.where(here & reach == 0, mine_first, theirs_first)]
    ppermute x0 -> x4, starting transfers between devices: none -> 7.41 us  [collect(): theirs = lax.ppermute(grown, axis, [(d, d ^ reach) for d in range(ways)])]
    transpose x0 -> x1, other arithmetic: none -> 4.14 us  [regroup(): return matrix.reshape(leading, across, along, piece_width).transpose(0, 2...]
  transfers between devices with their start and end apart: 16 -> 19, of which waited for: 14 -> 16; matrix products, arithmetic and copies ran while one was open for 5% -> 8% of each run, Pallas kernels for 0% -> 0%
where the time goes in v1:
time: 330 us; the launch traced here: 329 us
  waiting for transfers between devices  179 us (54%)
  blocking collectives  32.1 us (10%)
  matrix products  31 us (9%)
  other arithmetic  24.7 us (7%)
  starting transfers between devices  21.5 us (7%)
  between operations  20.7 us (6%)
  local copies, waits for them, and re-layouts  19.9 us (6%)
    ppermute x12, waiting for transfers between devices, passed_along(): lax.ppermute(shard, axis, [(i, (i + by) % devices) for i in range(devices)])  98.7 us
    ppermute x4, waiting for transfers between devices, collect(): theirs = lax.ppermute(grown, axis, [(d, d ^ reach) for d in range(ways)])  49.9 us
    all_gather x1, blocking collectives, per_device(): lax.all_gather(slice_part(mod_part, position, across), ('wrow', 'wcol'),...  32.1 us
    ppermute x2, waiting for transfers between devices, from_behind(): return lax.ppermute(shard, axis, pairs)  30.2 us
    dot_general x6, matrix products, project(): jnp.dot(region.reshape(tile_rows * tile_cols, feature_width), matrix, pre...  23.5 us
    select_n x4, other arithmetic, collect(): grown = jnp.where(here & reach == 0, mine_first, theirs_first)  8.76 us
    ppermute x2, starting transfers between devices, from_behind(): return lax.ppermute(shard, axis, pairs)  7.94 us
    ppermute x4, starting transfers between devices, collect(): theirs = lax.ppermute(grown, axis, [(d, d ^ reach) for d in range(ways)])  7.41 us
  transfers between devices with their start and end apart: 19, of which 16 were waited for; matrix products, arithmetic and copies ran while one was open for 8% of the time, Pallas kernels for 0%

profile of v1, /device:TPU:0, one launch (start us, length us, event | category | flops | bytes accessed | tf_op | source)
XLA Modules:
  0.0 328.7 jit_solution(13306286632382749068)
XLA Ops:
  8.0 3.1 collective-permute-start.2
  11.2 10.2 %collective-permute-done.2 = bf16[1536,144]{0,1:T(8,128)(2,1)S(1)} collective-permute-done((bf16[1536,144]{0,1:T(8,128)(2,1)S(1)}, bf16[1536,144]{0,1:T(8,128)(2,1)S(1)}, u32[]{:S(2)}, u32[]{:S(2)}) %collective-permute-start.2) | collective-permute-done | bytes 442400 | tf_op jit(solution)/shard_map/ppermute | solution.py:19
  21.5 2.8 collective-permute-start.3
  24.4 37.9 %collective-permute-done.3 = bf16[1536,288]{0,1:T(8,128)(2,1)S(1)} collective-permute-done((bf16[1536,288]{0,1:T(8,128)(2,1)S(1)}, bf16[1536,288]{0,1:T(8,128)(2,1)S(1)}, u32[]{:S(2)}, u32[]{:S(2)}) %collective-permute-start.3) | collective-permute-done | bytes 884768 | tf_op jit(solution)/shard_map/ppermute | solution.py:19
  66.8 3.8 %maximum_select_fusion.2 = bf16[1536,1152]{0,1:T(8,128)(2,1)} fusion(bf16[1536,576]{0,1:T(8,128)(2,1)} %collective-permute-done.4, bf16[1536,576]{0,1:T(8,128)(2,1)S(1)} %maximum_select_fusion.3, pred[]{:T(512)S(6)} %eq.19), kind=kLoop, calls=%fused_computation.6 | loop fusion | flops 15925248 | bytes 7077889 | tf_op jit(solution)/shard_map/jit(_where)/select_n | solution.py:22
  73.6 32.1 %all-gather.1 = bf16[16,288,2]{1,2,0:T(2,128)(2,1)S(1)} all-gather(bf16[1,288,2]{1,2,0:T(2,128)(2,1)S(1)} %fusion.63), channel_id=1, replica_groups=mesh['section'=2,'wrow'=4,'wcol'=4] {'wrow','wcol'}, dimensions={0}, use_global_device_ids=true | all-gather | bytes 19584 | tf_op jit(solution)/shard_map/all_gather | solution.py:150
  113.4 45.2 %collective-permute-done = bf16[4,16,1536]{2,1,0:T(8,128)(2,1)S(1)} collective-permute-done((bf16[4,16,1536]{2,1,0:T(8,128)(2,1)S(1)}, bf16[4,16,1536]{2,1,0:T(8,128)(2,1)S(1)}, u32[]{:S(2)}, u32[]{:S(2)}) %collective-permute-start) | collective-permute-done | bytes 196640 | tf_op jit(solution)/shard_map/ppermute | solution.py:29
  159.8 3.5 %collective-permute-start.1 = (bf16[16,4,1536]{2,1,0:T(4,128)(2,1)S(1)}, bf16[16,4,1536]{2,1,0:T(4,128)(2,1)S(1)}, u32[]{:S(2)}, u32[]{:S(2)}) collective-permute-start(bf16[16,4,1536]{2,1,0:T(4,128)(2,1)S(1)} %slice.177), channel_id=1, source_target_pairs={{0,3},{1,0},{2,1},{3,2},{4,7},{5,4},{6,5},{7,6},{8,11},{9,8},{10,9... | collective-permute-start | bytes 589832 | tf_op jit(solution)/shard_map/ppermute | solution.py:29
  163.4 4.1 %maximum_select_fusion.1 = bf16[1536,2,4,144]{0,3,2,1:T(8,128)(2,1)} fusion(bf16[1536,1,4,144]{0,3,2,1:T(8,128)(2,1)} %bitcast.10, bf16[1536,1,4,144]{0,3,2,1:T(8,128)(2,1)S(1)} %bitcast.131, pred[]{:T(512)S(6)} %eq.19), kind=kLoop, calls=%fused_computation.5 | loop fusion | flops 5308416 | bytes 7077889 | tf_op jit(solution)/shard_map/jit(_where)/select_n | solution.py:22
  167.4 3.4 %copy.61 = bf16[768,4,4,96]{0,3,2,1:T(8,128)(2,1)} copy(bf16[768,4,4,96]{0,3,1,2:T(8,128)(2,1)} %bitcast.139) | data formatting | bytes 4718592 | tf_op jit(solution)/shard_map/transpose | solution.py:132
  170.8 4.1 %fusion = bf16[1536,4,4,144]{0,3,1,2:T(8,128)(2,1)S(1)} fusion(bf16[1536,2,4,144]{0,3,2,1:T(8,128)(2,1)} %bitcast.11, bf16[1536,2,4,144]{0,3,2,1:T(8,128)(2,1)S(1)} %copy-done.2, pred[]{:T(512)S(6)} %eq.18), kind=kLoop, calls=%fused_computation.1 | loop fusion | flops 10616832 | bytes 14155777 | tf_op jit(solution)/shard_map/transpose | solution.py:132
  175.0 3.5 %copy.53 = bf16[1536,4,4,144]{0,3,2,1:T(8,128)(2,1)} copy(bf16[1536,4,4,144]{0,3,1,2:T(8,128)(2,1)S(1)} %fusion) | data formatting | bytes 14155776 | tf_op jit(solution)/shard_map/transpose | solution.py:132
  178.5 5.4 %convolution_convert_fusion.2 = bf16[16,16,2304]{2,1,0:T(8,128)(2,1)S(1)} fusion(bf16[1536,2304,1]{0,1,2:T(8,128)(2,1)} %bitcast.133, s32[]{:T(128)S(6)} %select_n.137, bf16[16,16,1536]{2,1,0:T(8,128)(2,1)S(1)} %fusion.32, bf16[16,4,1536]{2,1,0:T(4,128)(2,1)S(1)} %collective-permute-done.1), kind=kOutput, calls=%fused_computation.4 | convolution fusion | flops 1814102016 | bytes 9240580 | tf_op jit(solution)/shard_map/dot_general | solution.py:74
  189.4 3.3 %collective-permute-done.6 = bf16[4,16,1536]{2,1,0:T(8,128)(2,1)S(1)} collective-permute-done((bf16[4,16,1536]{2,1,0:T(8,128)(2,1)S(1)}, bf16[4,16,1536]{2,1,0:T(8,128)(2,1)S(1)}, u32[]{:S(2)}, u32[]{:S(2)}) %collective-permute-start.6) | collective-permute-done | bytes 196640 | tf_op jit(solution)/shard_map/ppermute | solution.py:29
  195.3 6.1 %collective-permute-done.7 = bf16[16,4,1536]{2,1,0:T(4,128)(2,1)S(1)} collective-permute-done((bf16[16,4,1536]{2,1,0:T(4,128)(2,1)S(1)}, bf16[16,4,1536]{2,1,0:T(4,128)(2,1)S(1)}, u32[]{:S(2)}, u32[]{:S(2)}) %collective-permute-start.7) | collective-permute-done | bytes 196640 | tf_op jit(solution)/shard_map/ppermute | solution.py:29
  202.3 3.5 %collective-permute-start.8 = (bf16[16,16,1536]{2,1,0:T(8,128)(2,1)S(1)}, bf16[16,16,1536]{2,1,0:T(8,128)(2,1)S(1)}, u32[]{:S(2)}, u32[]{:S(2)}) collective-permute-start(bf16[16,16,1536]{2,1,0:T(8,128)(2,1)S(1)} %get-tuple-element.21), channel_id=1, source_target_pairs={{0,16},{1,17},{2,18},{3,19},{4,20},{5,21},{6,22},{7,23},{8,24},{9,... | collective-permute-start | bytes 2359304 | tf_op jit(solution)/shard_map/ppermute | solution.py:35
  205.9 13.8 %collective-permute-done.8 = bf16[16,16,1536]{2,1,0:T(8,128)(2,1)S(1)} collective-permute-done((bf16[16,16,1536]{2,1,0:T(8,128)(2,1)S(1)}, bf16[16,16,1536]{2,1,0:T(8,128)(2,1)S(1)}, u32[]{:S(2)}, u32[]{:S(2)}) %collective-permute-start.8) | collective-permute-done | bytes 786464 | tf_op jit(solution)/shard_map/ppermute | solution.py:35
  220.9 3.2 collective-permute-done.9
  224.6 6.3 %collective-permute-done.10 = bf16[16,4,1536]{2,1,0:T(4,128)(2,1)S(1)} collective-permute-done((bf16[16,4,1536]{2,1,0:T(4,128)(2,1)S(1)}, bf16[16,4,1536]{2,1,0:T(4,128)(2,1)S(1)}, u32[]{:S(2)}, u32[]{:S(2)}) %collective-permute-start.10) | collective-permute-done | bytes 196640 | tf_op jit(solution)/shard_map/ppermute | solution.py:29
  230.9 5.4 %convolution_convert_fusion.1 = bf16[16,16,2304]{2,1,0:T(8,128)(2,1)S(1)} fusion(bf16[1536,2304,1]{0,1,2:T(8,128)(2,1)} %bitcast.134, s32[]{:T(128)S(6)} %select_n.137, bf16[16,16,1536]{2,1,0:T(8,128)(2,1)S(1)} %fusion.30, bf16[16,4,1536]{2,1,0:T(4,128)(2,1)S(1)} %collective-permute-done.10), kind=kOutput, calls=%fused_computation.3 | convolution fusion | flops 1814102016 | bytes 9240580 | tf_op jit(solution)/shard_map/dot_general | solution.py:74
  238.7 2.7 convolution_convert_fusion.7
  242.4 2.5 convolution_convert_fusion.4
  246.2 3.9 %collective-permute-done.11 = bf16[4,16,1536]{2,1,0:T(8,128)(2,1)S(1)} collective-permute-done((bf16[4,16,1536]{2,1,0:T(8,128)(2,1)S(1)}, bf16[4,16,1536]{2,1,0:T(8,128)(2,1)S(1)}, u32[]{:S(2)}, u32[]{:S(2)}) %collective-permute-start.11) | collective-permute-done | bytes 196640 | tf_op jit(solution)/shard_map/ppermute | solution.py:29
  251.2 9.0 %collective-permute-done.12 = bf16[16,4,1536]{2,1,0:T(4,128)(2,1)S(1)} collective-permute-done((bf16[16,4,1536]{2,1,0:T(4,128)(2,1)S(1)}, bf16[16,4,1536]{2,1,0:T(4,128)(2,1)S(1)}, u32[]{:S(2)}, u32[]{:S(2)}) %collective-permute-start.12) | collective-permute-done | bytes 196640 | tf_op jit(solution)/shard_map/ppermute | solution.py:29
  262.4 4.4 %collective-permute-start.13 = (bf16[16,16,1536]{2,1,0:T(8,128)(2,1)S(1)}, bf16[16,16,1536]{2,1,0:T(8,128)(2,1)S(1)}, u32[]{:S(2)}, u32[]{:S(2)}) collective-permute-start(bf16[16,16,1536]{2,1,0:T(8,128)(2,1)S(1)} %get-tuple-element.17), channel_id=1, source_target_pairs={{0,16},{1,17},{2,18},{3,19},{4,20},{5,21},{6,22},{7,23},{8,24},{9,... | collective-permute-start | bytes 2359304 | tf_op jit(solution)/shard_map/ppermute | solution.py:35
  266.9 16.4 %collective-permute-done.13 = bf16[16,16,1536]{2,1,0:T(8,128)(2,1)S(1)} collective-permute-done((bf16[16,16,1536]{2,1,0:T(8,128)(2,1)S(1)}, bf16[16,16,1536]{2,1,0:T(8,128)(2,1)S(1)}, u32[]{:S(2)}, u32[]{:S(2)}) %collective-permute-start.13) | collective-permute-done | bytes 786464 | tf_op jit(solution)/shard_map/ppermute | solution.py:35
  284.4 3.2 collective-permute-done.14
  288.0 7.3 %collective-permute-done.15 = bf16[16,4,1536]{2,1,0:T(4,128)(2,1)S(1)} collective-permute-done((bf16[16,4,1536]{2,1,0:T(4,128)(2,1)S(1)}, bf16[16,4,1536]{2,1,0:T(4,128)(2,1)S(1)}, u32[]{:S(2)}, u32[]{:S(2)}) %collective-permute-start.15) | collective-permute-done | bytes 196640 | tf_op jit(solution)/shard_map/ppermute | solution.py:29
  295.3 5.4 %convolution_convert_fusion = bf16[16,16,2304]{2,1,0:T(8,128)(2,1)S(1)} fusion(bf16[1536,2304,1]{0,1,2:T(8,128)(2,1)} %bitcast.135, s32[]{:T(128)S(6)} %select_n.137, bf16[16,16,1536]{2,1,0:T(8,128)(2,1)S(1)} %fusion.28, bf16[16,4,1536]{2,1,0:T(4,128)(2,1)S(1)} %collective-permute-done.15), kind=kOutput, calls=%fused_computation.2 | convolution fusion | flops 1814102016 | bytes 9240580 | tf_op jit(solution)/shard_map/dot_general | solution.py:74
  306.2 5.1 %collective-permute-done.16 = bf16[4,16,1536]{2,1,0:T(8,128)(2,1)S(1)} collective-permute-done((bf16[4,16,1536]{2,1,0:T(8,128)(2,1)S(1)}, bf16[4,16,1536]{2,1,0:T(8,128)(2,1)S(1)}, u32[]{:S(2)}, u32[]{:S(2)}) %collective-permute-start.16) | collective-permute-done | bytes 196640 | tf_op jit(solution)/shard_map/ppermute | solution.py:29
  312.8 6.2 %collective-permute-done.17 = bf16[16,4,1536]{2,1,0:T(4,128)(2,1)S(1)} collective-permute-done((bf16[16,4,1536]{2,1,0:T(4,128)(2,1)S(1)}, bf16[16,4,1536]{2,1,0:T(4,128)(2,1)S(1)}, u32[]{:S(2)}, u32[]{:S(2)}) %collective-permute-start.17) | collective-permute-done | bytes 196640 | tf_op jit(solution)/shard_map/ppermute | solution.py:29
  319.0 2.8 fusion.45
  (130 shorter events, 38.5 us)
Async XLA Ops:
  6.5 1.5 copy-start
  6.5 160.9 %all-gather.4.cloned.1.call-start = ((), (), s32[]{:S(2)}) async-start(), calls=%async_computation | async-start | bytes 2506752 | tf_op jit(solution)/shard_map/all_gather | solution.py:147
  8.0 13.3 %collective-permute-start.2 = (bf16[1536,144]{0,1:T(8,128)(2,1)S(1)}, bf16[1536,144]{0,1:T(8,128)(2,1)S(1)}, u32[]{:S(2)}, u32[]{:S(2)}) collective-permute-start(bf16[1536,144]{0,1:T(8,128)(2,1)S(1)} %dynamic-slice_bitcast_fusion), channel_id=1, source_target_pairs={{0,1},{1,0},{2,3},{3,2},{4,5},{5,4},{6,7},{7,6},{8,9},{9,8},{10,11... | collective-permute-start | bytes 1327112 | tf_op jit(solution)/shard_map/ppermute | solution.py:19
  21.5 40.7 %collective-permute-start.3 = (bf16[1536,288]{0,1:T(8,128)(2,1)S(1)}, bf16[1536,288]{0,1:T(8,128)(2,1)S(1)}, u32[]{:S(2)}, u32[]{:S(2)}) collective-permute-start(bf16[1536,288]{0,1:T(8,128)(2,1)S(1)} %maximum_select_fusion.4), channel_id=1, source_target_pairs={{0,2},{1,3},{2,0},{3,1},{4,6},{5,7},{6,4},{7,5},{8,10},{9,11},{10,... | collective-permute-start | bytes 2654216 | tf_op jit(solution)/shard_map/ppermute | solution.py:19
  63.0 3.9 %collective-permute-start.4 = (bf16[1536,576]{0,1:T(8,128)(2,1)S(1)}, bf16[1536,576]{0,1:T(8,128)(2,1)}, u32[]{:S(2)}, u32[]{:S(2)}) collective-permute-start(bf16[1536,576]{0,1:T(8,128)(2,1)S(1)} %maximum_select_fusion.3), channel_id=1, source_target_pairs={{0,4},{1,5},{2,6},{3,7},{4,0},{5,1},{6,2},{7,3},{8,12},{9,13},{10,... | collective-permute-start | bytes 5308424 | tf_op jit(solution)/shard_map/ppermute | solution.py:19
  65.0 7.1 %copy-start.15 = (s32[2]{0:T(128)S(1)}, s32[2]{0:T(128)}, u32[]{:S(2)}) copy-start(s32[2]{0:T(128)} %param.7) | copy-start | bytes 28
  66.8 39.9 %copy-start.3 = (bf16[2,16,16,1536]{3,2,1,0:T(8,128)(2,1)S(1)}, bf16[2,16,16,1536]{3,2,1,0:T(8,128)(2,1)}, u32[]{:S(2)}) copy-start(bf16[2,16,16,1536]{3,2,1,0:T(8,128)(2,1)} %param.6) | copy-start | bytes 4718596
  70.7 100.2 %collective-permute-start.5 = (bf16[1536,1152]{0,1:T(8,128)(2,1)}, bf16[1536,1152]{0,1:T(8,128)(2,1)}, u32[]{:S(2)}, u32[]{:S(2)}) collective-permute-start(bf16[1536,1152]{0,1:T(8,128)(2,1)} %maximum_select_fusion.2), channel_id=1, source_target_pairs={{0,8},{1,9},{2,10},{3,11},{4,12},{5,13},{6,14},{7,15},{8,0},{9,1},... | collective-permute-start | bytes 10616840 | tf_op jit(solution)/shard_map/ppermute | solution.py:19
  107.0 1.7 copy-start.14
  108.7 49.8 %collective-permute-start = (bf16[4,16,1536]{2,1,0:T(8,128)(2,1)S(1)}, bf16[4,16,1536]{2,1,0:T(8,128)(2,1)S(1)}, u32[]{:S(2)}, u32[]{:S(2)}) collective-permute-start(bf16[4,16,1536]{2,1,0:T(8,128)(2,1)S(1)} %slice.176), channel_id=1, source_target_pairs={{0,12},{4,0},{8,4},{12,8},{1,13},{5,1},{9,5},{13,9},{2,14},{6,2},{... | collective-permute-start | bytes 589832 | tf_op jit(solution)/shard_map/ppermute | solution.py:29
  159.8 18.7 %collective-permute-start.1 = (bf16[16,4,1536]{2,1,0:T(4,128)(2,1)S(1)}, bf16[16,4,1536]{2,1,0:T(4,128)(2,1)S(1)}, u32[]{:S(2)}, u32[]{:S(2)}) collective-permute-start(bf16[16,4,1536]{2,1,0:T(4,128)(2,1)S(1)} %slice.177), channel_id=1, source_target_pairs={{0,3},{1,0},{2,1},{3,2},{4,7},{5,4},{6,5},{7,6},{8,11},{9,8},{10,9... | collective-permute-start | bytes 589832 | tf_op jit(solution)/shard_map/ppermute | solution.py:29
  167.4 3.4 %copy-start.2 = (bf16[1536,2,4,144]{0,3,2,1:T(8,128)(2,1)S(1)}, bf16[1536,2,4,144]{0,3,2,1:T(8,128)(2,1)}, u32[]{:S(2)}) copy-start(bf16[1536,2,4,144]{0,3,2,1:T(8,128)(2,1)} %maximum_select_fusion.1) | copy-start | bytes 10616836
  187.5 5.1 %collective-permute-start.6 = (bf16[4,16,1536]{2,1,0:T(8,128)(2,1)S(1)}, bf16[4,16,1536]{2,1,0:T(8,128)(2,1)S(1)}, u32[]{:S(2)}, u32[]{:S(2)}) collective-permute-start(bf16[4,16,1536]{2,1,0:T(8,128)(2,1)S(1)} %slice.181), channel_id=1, source_target_pairs={{0,4},{4,8},{8,12},{12,0},{1,5},{5,9},{9,13},{13,1},{2,6},{6,10},{... | collective-permute-start | bytes 589832 | tf_op jit(solution)/shard_map/ppermute | solution.py:29
  189.4 12.1 %copy-start.4 = (bf16[2,16,16,1536]{3,2,1,0:T(8,128)(2,1)S(1)}, bf16[2,16,16,1536]{3,2,1,0:T(8,128)(2,1)}, u32[]{:S(2)}) copy-start(bf16[2,16,16,1536]{3,2,1,0:T(8,128)(2,1)} %param.6) | copy-start | bytes 4718596
  193.8 7.5 %collective-permute-start.7 = (bf16[16,4,1536]{2,1,0:T(4,128)(2,1)S(1)}, bf16[16,4,1536]{2,1,0:T(4,128)(2,1)S(1)}, u32[]{:S(2)}, u32[]{:S(2)}) collective-permute-start(bf16[16,4,1536]{2,1,0:T(4,128)(2,1)S(1)} %slice.182), channel_id=1, source_target_pairs={{0,1},{1,2},{2,3},{3,0},{4,5},{5,6},{6,7},{7,4},{8,9},{9,10},{10,1... | collective-permute-start | bytes 589832 | tf_op jit(solution)/shard_map/ppermute | solution.py:29
  195.3 6.3 %copy-start.11 = (bf16[16,16,1536]{2,1,0:T(8,128)(2,1)S(1)}, bf16[16,16,1536]{2,1,0:T(8,128)(2,1)}, u32[]{:S(2)}) copy-start(bf16[16,16,1536]{2,1,0:T(8,128)(2,1)} %copy-done.10) | copy-start | bytes 2359300
  202.3 17.4 %collective-permute-start.8 = (bf16[16,16,1536]{2,1,0:T(8,128)(2,1)S(1)}, bf16[16,16,1536]{2,1,0:T(8,128)(2,1)S(1)}, u32[]{:S(2)}, u32[]{:S(2)}) collective-permute-start(bf16[16,16,1536]{2,1,0:T(8,128)(2,1)S(1)} %get-tuple-element.21), channel_id=1, source_target_pairs={{0,16},{1,17},{2,18},{3,19},{4,20},{5,21},{6,22},{7,23},{8,24},{9,... | collective-permute-start | bytes 2359304 | tf_op jit(solution)/shard_map/ppermute | solution.py:35
  220.0 4.3 %copy-start.5 = (bf16[16,16,1536]{2,1,0:T(8,128)(2,1)}, bf16[16,16,1536]{2,1,0:T(8,128)(2,1)S(1)}, u32[]{:S(2)}) copy-start(bf16[16,16,1536]{2,1,0:T(8,128)(2,1)S(1)} %get-tuple-element.19) | copy-start | bytes 2359300
  220.8 3.2 collective-permute-start.9
  224.3 6.6 %collective-permute-start.10 = (bf16[16,4,1536]{2,1,0:T(4,128)(2,1)S(1)}, bf16[16,4,1536]{2,1,0:T(4,128)(2,1)S(1)}, u32[]{:S(2)}, u32[]{:S(2)}) collective-permute-start(bf16[16,4,1536]{2,1,0:T(4,128)(2,1)S(1)} %slice.187), channel_id=1, source_target_pairs={{0,3},{1,0},{2,1},{3,2},{4,7},{5,4},{6,5},{7,6},{8,11},{9,8},{10,9... | collective-permute-start | bytes 589832 | tf_op jit(solution)/shard_map/ppermute | solution.py:29
  244.9 5.1 %collective-permute-start.11 = (bf16[4,16,1536]{2,1,0:T(8,128)(2,1)S(1)}, bf16[4,16,1536]{2,1,0:T(8,128)(2,1)S(1)}, u32[]{:S(2)}, u32[]{:S(2)}) collective-permute-start(bf16[4,16,1536]{2,1,0:T(8,128)(2,1)S(1)} %slice.191), channel_id=1, source_target_pairs={{0,4},{4,8},{8,12},{12,0},{1,5},{5,9},{9,13},{13,1},{2,6},{6,10},{... | collective-permute-start | bytes 589832 | tf_op jit(solution)/shard_map/ppermute | solution.py:29
  251.2 9.0 %collective-permute-start.12 = (bf16[16,4,1536]{2,1,0:T(4,128)(2,1)S(1)}, bf16[16,4,1536]{2,1,0:T(4,128)(2,1)S(1)}, u32[]{:S(2)}, u32[]{:S(2)}) collective-permute-start(bf16[16,4,1536]{2,1,0:T(4,128)(2,1)S(1)} %slice.192), channel_id=1, source_target_pairs={{0,1},{1,2},{2,3},{3,0},{4,5},{5,6},{6,7},{7,4},{8,9},{9,10},{10,1... | collective-permute-start | bytes 589832 | tf_op jit(solution)/shard_map/ppermute | solution.py:29
  260.2 6.7 %copy-start.13 = (f32[1,4608]{1,0:T(1,128)S(1)}, f32[1,4608]{1,0:T(1,128)}, u32[]{:S(2)}) copy-start(f32[1,4608]{1,0:T(1,128)} %get-tuple-element.31) | copy-start | bytes 55300
  262.4 20.9 %collective-permute-start.13 = (bf16[16,16,1536]{2,1,0:T(8,128)(2,1)S(1)}, bf16[16,16,1536]{2,1,0:T(8,128)(2,1)S(1)}, u32[]{:S(2)}, u32[]{:S(2)}) collective-permute-start(bf16[16,16,1536]{2,1,0:T(8,128)(2,1)S(1)} %get-tuple-element.17), channel_id=1, source_target_pairs={{0,16},{1,17},{2,18},{3,19},{4,20},{5,21},{6,22},{7,23},{8,24},{9,... | collective-permute-start | bytes 2359304 | tf_op jit(solution)/shard_map/ppermute | solution.py:35
  283.6 4.3 %copy-start.6 = (bf16[16,16,1536]{2,1,0:T(8,128)(2,1)}, bf16[16,16,1536]{2,1,0:T(8,128)(2,1)S(1)}, u32[]{:S(2)}) copy-start(bf16[16,16,1536]{2,1,0:T(8,128)(2,1)S(1)} %get-tuple-element.15) | copy-start | bytes 2359300
  284.4 3.2 collective-permute-start.14
  287.9 7.4 %collective-permute-start.15 = (bf16[16,4,1536]{2,1,0:T(4,128)(2,1)S(1)}, bf16[16,4,1536]{2,1,0:T(4,128)(2,1)S(1)}, u32[]{:S(2)}, u32[]{:S(2)}) collective-permute-start(bf16[16,4,1536]{2,1,0:T(4,128)(2,1)S(1)} %slice.197), channel_id=1, source_target_pairs={{0,3},{1,0},{2,1},{3,2},{4,7},{5,4},{6,5},{7,6},{8,11},{9,8},{10,9... | collective-permute-start | bytes 589832 | tf_op jit(solution)/shard_map/ppermute | solution.py:29
  306.1 5.1 %collective-permute-start.16 = (bf16[4,16,1536]{2,1,0:T(8,128)(2,1)S(1)}, bf16[4,16,1536]{2,1,0:T(8,128)(2,1)S(1)}, u32[]{:S(2)}, u32[]{:S(2)}) collective-permute-start(bf16[4,16,1536]{2,1,0:T(8,128)(2,1)S(1)} %slice.201), channel_id=1, source_target_pairs={{0,4},{4,8},{8,12},{12,0},{1,5},{5,9},{9,13},{13,1},{2,6},{6,10},{... | collective-permute-start | bytes 589832 | tf_op jit(solution)/shard_map/ppermute | solution.py:29
  311.4 1.4 copy-start.12
  311.5 7.5 %collective-permute-start.17 = (bf16[16,4,1536]{2,1,0:T(4,128)(2,1)S(1)}, bf16[16,4,1536]{2,1,0:T(4,128)(2,1)S(1)}, u32[]{:S(2)}, u32[]{:S(2)}) collective-permute-start(bf16[16,4,1536]{2,1,0:T(4,128)(2,1)S(1)} %slice.202), channel_id=1, source_target_pairs={{0,1},{1,2},{2,3},{3,0},{4,5},{5,6},{6,7},{7,4},{8,9},{9,10},{10,1... | collective-permute-start | bytes 589832 | tf_op jit(solution)/shard_map/ppermute | solution.py:29
  311.6 7.5 %copy-start.7 = (bf16[16,16,1536]{2,1,0:T(8,128)(2,1)S(1)}, bf16[16,16,1536]{2,1,0:T(8,128)(2,1)}, u32[]{:S(2)}) copy-start(bf16[16,16,1536]{2,1,0:T(8,128)(2,1)} %copy-done.6) | copy-start | bytes 2359300
  319.0 2.9 copy-start.1
  (3 other events, 2.6 us)
Sparse Core Ops, SparseCore 0:
  65.1 49.8 all-gather.3
